TPU v7x, 512 devices: a whole 4x8x8 slice. The times are simulated.
512 devices in a mesh: lon: 64 (over x, y_hi, z), lat: 8 (over y_lo, core).
Axes of the slice: x: 4, y: 8 (y_hi: 2, y_lo: 4; y = y_hi * 4 + y_lo), z: 8, core: 2. Of those that a mesh axis runs over, the one named last changes fastest.
Arguments:
- fields: bfloat16 [2048, 512, 256], P('lon', 'lat'), may hold values from -48 to 48
Outputs:
- coarse_fluxes: bfloat16 [2048, 512, 256], P('lon', 'lat')
- snapshot_gram: float32 [64, 64], replicated
All inputs are finite; a program needn't handle non-finite values.
Results may differ from a plain program's by a relative error of at most 0.0064.
Values may be sent and summed in bfloat16 or wider, within the bound.
A program may use at most 64 MiB of HBM per device.

v0:
```python
import jax
import jax.numpy as jnp
from jax import lax
from jax.sharding import Mesh
from jax.sharding import PartitionSpec as P

R = 128
LON = ("lon_0", "lon_1", "lon_2")
LAT = ("lat_0", "lat_1")
LON_LAT = ("lon_0", "lon_1", "lon_2", "lat_0", "lat_1")


def from_behind(shard, axis, by):
    peers = lax.axis_size(axis)
    pairs = [(i, i + by) for i in range(peers) if 0 <= i + by < peers]
    return lax.ppermute(shard, axis, pairs)


def by_axis(shard, axes):
    for axis in axes:
        shard = lax.psum(shard, axis)
    return shard


def tap_block(row_count, col_count, offset):
    row_ids = lax.broadcasted_iota(jnp.int32, (row_count, col_count), 0)
    col_ids = lax.broadcasted_iota(jnp.int32, (row_count, col_count), 1)
    distance = col_ids - row_ids + offset
    weight = jnp.exp(-((distance.astype(jnp.float32) / R) ** 2))
    return jnp.where(jnp.abs(distance) <= R, weight, 0.0).astype(jnp.bfloat16)


def flux_products(values, snapshots):
    left_side = jnp.concatenate([values[:, :, : 3 * snapshots], values[:, :, :snapshots]], axis=2)
    right_side = jnp.concatenate(
        [values[:, :, 3 * snapshots :]] * 3 + [values[:, :, snapshots : 2 * snapshots]], axis=2
    )
    return (left_side.astype(jnp.float32) * right_side.astype(jnp.float32)).astype(jnp.bfloat16)


def shards(fields):
    lon_cells, lat_cells, channels = fields.shape
    snapshots = channels // 4
    total_lon = lon_cells * lax.axis_size(LON)
    total_lat = lat_cells * lax.axis_size(LAT)
    products = flux_products(fields, snapshots)
    flattened = products.reshape(lon_cells, lat_cells * channels)
    lon_norm = jnp.sum(tap_block(1, 2 * R + 1, -R).astype(jnp.float32))
    cycle_rows = lax.all_to_all(flattened, LON, split_axis=1, concat_axis=0, tiled=True)
    blocks = cycle_rows.reshape(total_lon // R, R, cycle_rows.shape[1])
    near_taps = tap_block(R, 3 * R, -R)
    summed = jnp.einsum(
        "ij,bjk->bik", near_taps[:, R : 2 * R], blocks, preferred_element_type=jnp.float32
    )
    summed = summed + jnp.einsum(
        "ij,bjk->bik", near_taps[:, :R], jnp.roll(blocks, 1, 0), preferred_element_type=jnp.float32
    )
    summed = summed + jnp.einsum(
        "ij,bjk->bik",
        near_taps[:, 2 * R :],
        jnp.roll(blocks, -1, 0),
        preferred_element_type=jnp.float32,
    )
    filtered = (summed / lon_norm).astype(jnp.bfloat16).reshape(total_lon, cycle_rows.shape[1])
    lon_done = lax.all_to_all(filtered, LON, split_axis=0, concat_axis=1, tiled=True)
    smoothed = lon_done.reshape(lon_cells, lat_cells, channels)
    row_start = lax.axis_index(LAT) * lat_cells
    lat_weights = tap_block(lat_cells, total_lat, -row_start).astype(jnp.float32)
    lat_norm = jnp.sum(lat_weights, axis=1)
    reach_count = -(-R // lat_cells)
    summed = jnp.einsum(
        "ij,xjc->xic",
        tap_block(lat_cells, lat_cells, 0),
        smoothed,
        preferred_element_type=jnp.float32,
    )
    shift_list = [sign * depth for depth in range(1, reach_count + 1) for sign in (1, -1)]
    for offset_by in shift_list:
        shard_piece = from_behind(smoothed, LAT, offset_by)
        summed = summed + jnp.einsum(
            "ij,xjc->xic",
            tap_block(lat_cells, lat_cells, -offset_by * lat_cells),
            shard_piece,
            preferred_element_type=jnp.float32,
        )
    coarse_fluxes = (summed / lat_norm[None, :, None]).astype(jnp.bfloat16)
    rows_flat = coarse_fluxes.reshape(-1, snapshots)
    partial_gram = lax.dot_general(
        rows_flat, rows_flat, (((0,), (0,)), ((), ())), preferred_element_type=jnp.float32
    )
    snapshot_gram = by_axis(partial_gram, LON_LAT) / (4 * total_lon * total_lat)
    return (coarse_fluxes, snapshot_gram)


def solution(mesh):
    split = Mesh(mesh.devices.reshape(4, 2, 8, 4, 2), ("lon_0", "lon_1", "lon_2", "lat_0", "lat_1"))
    in_specs = (P(LON, LAT, None),)
    out_specs = (P(LON, LAT, None), P())
    return jax.shard_map(
        shards, mesh=split, in_specs=in_specs, out_specs=out_specs, check_vma=False
    )
```

profile of v0, /device:TPU:1, one launch (start us, length us, event | category | flops | bytes accessed | tf_op | source)
XLA Modules:
  0.0 222.7 jit_solution(15256719595227012851)
XLA Ops:
  0.6 1.8 fusion.69
  2.4 0.3 copy.26
  2.8 0.3 copy.27
  3.6 0.6 copy.25
  4.2 2.0 multiply_convert_fusion
  6.2 19.6 %all-to-all-start = ((bf16[32,64,256]{2,0,1:T(8,128)(2,1)}), bf16[32,64,256]{2,0,1:T(8,128)(2,1)S(1)}, u32[]{:S(2)}, u32[]{:S(2)}) async-start(bf16[32,64,256]{2,0,1:T(8,128)(2,1)} %multiply_convert_fusion), calls=%async_computation | async-start | bytes 2097152 | tf_op jit(solution)/shard_map/all_to_all | solution.py:49
  25.8 0.6 fusion.46
  26.5 25.4 %all-to-all-done = bf16[32,64,256]{2,0,1:T(8,128)(2,1)S(1)} async-done(((bf16[32,64,256]{2,0,1:T(8,128)(2,1)}), bf16[32,64,256]{2,0,1:T(8,128)(2,1)S(1)}, u32[]{:S(2)}, u32[]{:S(2)}) %all-to-all-start) | async-done | bytes 1048608 | tf_op jit(solution)/shard_map/all_to_all | solution.py:49
  52.2 0.4 fusion.8
  52.6 0.4 fusion
  53.0 1.1 divide_convert_fusion.1
  54.1 43.6 %all_to_all.29 = bf16[64,32,256]{2,1,0:T(8,128)(2,1)S(1)} all-to-all(bf16[64,32,256]{2,1,0:T(8,128)(2,1)S(1)} %bitcast.55), channel_id=1, replica_groups=mesh['lon_0'=4,'lon_1'=2,'lon_2'=8,'lat_0'=4,'lat_1'=2] {'lon_0','lon_1'..., dimensions={0} | all-to-all | bytes 2097152 | tf_op jit(solution)/shard_map/all_to_all | solution.py:65
  97.8 1.6 copy.31
  99.3 6.6 %collective-permute-start.2 = (bf16[32,64,256]{2,1,0:T(8,128)(2,1)}, bf16[32,64,256]{2,1,0:T(8,128)(2,1)}, u32[]{:S(2)}, u32[]{:S(2)}) collective-permute-start(bf16[32,64,256]{2,1,0:T(8,128)(2,1)} %bitcast.48), channel_id=1, source_target_pairs={{0,2},{1,3},{2,4},{3,5},{4,6},{5,7},{8,10},{9,11},{10,12},{11,13},... | collective-permute-start | bytes 3145736 | tf_op jit(solution)/shard_map/ppermute | solution.py:16
  106.0 3.3 %collective-permute-start.1 = (bf16[32,64,256]{2,1,0:T(8,128)(2,1)}, bf16[32,64,256]{2,1,0:T(8,128)(2,1)S(1)}, u32[]{:S(2)}, u32[]{:S(2)}) collective-permute-start(bf16[32,64,256]{2,1,0:T(8,128)(2,1)} %bitcast.48), channel_id=1, source_target_pairs={{1,0},{2,1},{3,2},{4,3},{5,4},{6,5},{7,6},{9,8},{10,9},{11,10},{12... | collective-permute-start | bytes 3145736 | tf_op jit(solution)/shard_map/ppermute | solution.py:16
  109.3 2.2 collective-permute-start
  111.7 1.3 collective-permute-start.3
  113.0 0.9 fusion.20
  113.9 12.7 %collective-permute-done.2 = bf16[32,64,256]{2,1,0:T(8,128)(2,1)} collective-permute-done((bf16[32,64,256]{2,1,0:T(8,128)(2,1)}, bf16[32,64,256]{2,1,0:T(8,128)(2,1)}, u32[]{:S(2)}, u32[]{:S(2)}) %collective-permute-start.2) | collective-permute-done | bytes 1048608 | tf_op jit(solution)/shard_map/ppermute | solution.py:16
  126.6 1.6 fusion.14
  128.3 0.4 fusion.16
  128.8 10.7 %collective-permute-done = bf16[32,64,256]{2,1,0:T(8,128)(2,1)S(1)} collective-permute-done((bf16[32,64,256]{2,1,0:T(8,128)(2,1)}, bf16[32,64,256]{2,1,0:T(8,128)(2,1)S(1)}, u32[]{:S(2)}, u32[]{:S(2)}) %collective-permute-start) | collective-permute-done | bytes 1048608 | tf_op jit(solution)/shard_map/ppermute | solution.py:16
  139.5 0.4 fusion.18
  139.9 0.7 fusion.7
  140.6 0.9 reshape.78
  141.5 0.7 fusion.70
  142.2 11.6 %psum.35 = f32[64,64]{1,0:T(8,128)S(1)} all-reduce(f32[64,64]{1,0:T(8,128)S(1)} %fusion.70), channel_id=1, replica_groups=mesh['lon_0'=4,'lon_1'=2,'lon_2'=8,'lat_0'=4,'lat_1'=2] {'lon_0'}, use_global_device_ids=true, to_apply=%region_2.3 | all-reduce | flops 4096 | bytes 32768 | tf_op jit(solution)/shard_map/psum | solution.py:21
  153.8 9.1 %psum.36 = f32[64,64]{1,0:T(8,128)S(1)} all-reduce(f32[64,64]{1,0:T(8,128)S(1)} %psum.35), channel_id=1, replica_groups=mesh['lon_0'=4,'lon_1'=2,'lon_2'=8,'lat_0'=4,'lat_1'=2] {'lon_1'}, use_global_device_ids=true, to_apply=%region_3.4 | all-reduce | flops 4096 | bytes 32768 | tf_op jit(solution)/shard_map/psum | solution.py:21
  162.9 22.3 %psum.37 = f32[64,64]{1,0:T(8,128)S(1)} all-reduce(f32[64,64]{1,0:T(8,128)S(1)} %psum.36), channel_id=1, replica_groups=mesh['lon_0'=4,'lon_1'=2,'lon_2'=8,'lat_0'=4,'lat_1'=2] {'lon_2'}, use_global_device_ids=true, to_apply=%region_4.5 | all-reduce | flops 4096 | bytes 32768 | tf_op jit(solution)/shard_map/psum | solution.py:21
  185.3 12.4 %psum.38 = f32[64,64]{1,0:T(8,128)S(1)} all-reduce(f32[64,64]{1,0:T(8,128)S(1)} %psum.37), channel_id=1, replica_groups=mesh['lon_0'=4,'lon_1'=2,'lon_2'=8,'lat_0'=4,'lat_1'=2] {'lat_0'}, use_global_device_ids=true, to_apply=%region_5.6 | all-reduce | flops 4096 | bytes 32768 | tf_op jit(solution)/shard_map/psum | solution.py:21
  197.7 24.4 %psum.39 = f32[64,64]{1,0:T(8,128)S(1)} all-reduce(f32[64,64]{1,0:T(8,128)S(1)} %psum.38), channel_id=1, replica_groups=mesh['lon_0'=4,'lon_1'=2,'lon_2'=8,'lat_0'=4,'lat_1'=2] {'lat_1'}, use_global_device_ids=true, to_apply=%region_6.7 | all-reduce | flops 4096 | bytes 32768 | tf_op jit(solution)/shard_map/psum | solution.py:21
  222.1 0.6 broadcast_multiply_fusion
  (11 shorter events, 1.1 us)
Async XLA Ops:
  2.4 1.2 copy-start
  6.2 45.7 %all-to-all-start = ((bf16[32,64,256]{2,0,1:T(8,128)(2,1)}), bf16[32,64,256]{2,0,1:T(8,128)(2,1)S(1)}, u32[]{:S(2)}, u32[]{:S(2)}) async-start(bf16[32,64,256]{2,0,1:T(8,128)(2,1)} %multiply_convert_fusion), calls=%async_computation | async-start | bytes 2097152 | tf_op jit(solution)/shard_map/all_to_all | solution.py:49
  99.3 27.3 %collective-permute-start.2 = (bf16[32,64,256]{2,1,0:T(8,128)(2,1)}, bf16[32,64,256]{2,1,0:T(8,128)(2,1)}, u32[]{:S(2)}, u32[]{:S(2)}) collective-permute-start(bf16[32,64,256]{2,1,0:T(8,128)(2,1)} %bitcast.48), channel_id=1, source_target_pairs={{0,2},{1,3},{2,4},{3,5},{4,6},{5,7},{8,10},{9,11},{10,12},{11,13},... | collective-permute-start | bytes 3145736 | tf_op jit(solution)/shard_map/ppermute | solution.py:16
  106.0 22.4 %collective-permute-start.1 = (bf16[32,64,256]{2,1,0:T(8,128)(2,1)}, bf16[32,64,256]{2,1,0:T(8,128)(2,1)S(1)}, u32[]{:S(2)}, u32[]{:S(2)}) collective-permute-start(bf16[32,64,256]{2,1,0:T(8,128)(2,1)} %bitcast.48), channel_id=1, source_target_pairs={{1,0},{2,1},{3,2},{4,3},{5,4},{6,5},{7,6},{9,8},{10,9},{11,10},{12... | collective-permute-start | bytes 3145736 | tf_op jit(solution)/shard_map/ppermute | solution.py:16
  109.3 30.2 %collective-permute-start = (bf16[32,64,256]{2,1,0:T(8,128)(2,1)}, bf16[32,64,256]{2,1,0:T(8,128)(2,1)S(1)}, u32[]{:S(2)}, u32[]{:S(2)}) collective-permute-start(bf16[32,64,256]{2,1,0:T(8,128)(2,1)} %bitcast.48), channel_id=1, source_target_pairs={{0,1},{1,2},{2,3},{3,4},{4,5},{5,6},{6,7},{8,9},{9,10},{10,11},{11... | collective-permute-start | bytes 3145736 | tf_op jit(solution)/shard_map/ppermute | solution.py:16
  111.7 28.2 %collective-permute-start.3 = (bf16[32,64,256]{2,1,0:T(8,128)(2,1)}, bf16[32,64,256]{2,1,0:T(8,128)(2,1)S(1)}, u32[]{:S(2)}, u32[]{:S(2)}) collective-permute-start(bf16[32,64,256]{2,1,0:T(8,128)(2,1)} %bitcast.48), channel_id=1, source_target_pairs={{2,0},{3,1},{4,2},{5,3},{6,4},{7,5},{10,8},{11,9},{12,10},{13,11},... | collective-permute-start | bytes 3145736 | tf_op jit(solution)/shard_map/ppermute | solution.py:16
  140.6 1.6 copy-start.1
where the time goes:
time: 223 us
  blocking collectives  123 us (55%)
  waiting for transfers between devices  48.9 us (22%)
  starting transfers between devices  33.1 us (15%)
  matrix products  6.75 us (3%)
  local copies, waits for them, and re-layouts  6.22 us (3%)
  other arithmetic  3.49 us (2%)
    psum x5, blocking collectives, by_axis(): shard = lax.psum(shard, axis)  79.8 us
    all_to_all x1, blocking collectives, shards(): lax.all_to_all(filtered, LON, split_axis=0, concat_axis=1, tiled=True)  43.6 us
    all_to_all x1, waiting for transfers between devices, shards(): lax.all_to_all(flattened, LON, split_axis=1, concat_axis=0, tiled=True)  25.4 us
    ppermute x4, waiting for transfers between devices, from_behind(): return lax.ppermute(shard, axis, pairs)  23.5 us
    all_to_all x1, starting transfers between devices, shards(): lax.all_to_all(flattened, LON, split_axis=1, concat_axis=0, tiled=True)  19.6 us
    ppermute x4, starting transfers between devices, from_behind(): return lax.ppermute(shard, axis, pairs)  13.5 us
  transfers between devices with their start and end apart: 5, of which 4 were waited for; matrix products, arithmetic and copies ran while one was open for 2% of the time, Pallas kernels for 0%

commit v1 on v0

--- a/solution.py
+++ b/solution.py
@@ -18,7 +18,7 @@
 
 def by_axis(shard, axes):
     for axis in axes:
-        shard = lax.psum(shard, axis)
+        shard = jnp.sum(lax.all_gather(shard, axis), axis=0)
     return shard
 
 

time: 223 us -> 209 us (0.937)
  blocking collectives: 123 us -> 109 us
    psum x5 -> x0, blocking collectives: 79.8 us -> none  [by_axis(): shard = lax.psum(shard, axis)]
    all_gather x0 -> x5, blocking collectives: none -> 65.8 us  [by_axis(): shard = jnp.sum(lax.all_gather(shard, axis), axis=0)]
where the time goes in v1:
time: 209 us
  blocking collectives  109 us (52%)
  waiting for transfers between devices  48.9 us (23%)
  starting transfers between devices  33.1 us (16%)
  matrix products  6.75 us (3%)
  local copies, waits for them, and re-layouts  6.22 us (3%)
  other arithmetic  3.56 us (2%)
    all_gather x5, blocking collectives, by_axis(): shard = jnp.sum(lax.all_gather(shard, axis), axis=0)  65.8 us
    all_to_all x1, blocking collectives, shards(): lax.all_to_all(filtered, LON, split_axis=0, concat_axis=1, tiled=True)  43.6 us
    all_to_all x1, waiting for transfers between devices, shards(): lax.all_to_all(flattened, LON, split_axis=1, concat_axis=0, tiled=True)  25.4 us
    ppermute x4, waiting for transfers between devices, from_behind(): return lax.ppermute(shard, axis, pairs)  23.5 us
    all_to_all x1, starting transfers between devices, shards(): lax.all_to_all(flattened, LON, split_axis=1, concat_axis=0, tiled=True)  19.6 us
    ppermute x4, starting transfers between devices, from_behind(): return lax.ppermute(shard, axis, pairs)  13.5 us
  transfers between devices with their start and end apart: 5, of which 4 were waited for; matrix products, arithmetic and copies ran while one was open for 2% of the time, Pallas kernels for 0%

profile of v1, /device:TPU:1, one launch (start us, length us, event | category | flops | bytes accessed | tf_op | source)
XLA Modules:
  0.0 208.7 jit_solution(8482923024240621844)
XLA Ops:
  0.6 1.8 fusion.69
  2.4 0.3 copy.26
  2.8 0.3 copy.27
  3.6 0.6 copy.25
  4.2 2.0 multiply_convert_fusion
  6.2 19.6 %all-to-all-start = ((bf16[32,64,256]{2,0,1:T(8,128)(2,1)}), bf16[32,64,256]{2,0,1:T(8,128)(2,1)S(1)}, u32[]{:S(2)}, u32[]{:S(2)}) async-start(bf16[32,64,256]{2,0,1:T(8,128)(2,1)} %multiply_convert_fusion), calls=%async_computation | async-start | bytes 2097152 | tf_op jit(solution)/shard_map/all_to_all | solution.py:49
  25.8 0.6 fusion.46
  26.5 25.4 %all-to-all-done = bf16[32,64,256]{2,0,1:T(8,128)(2,1)S(1)} async-done(((bf16[32,64,256]{2,0,1:T(8,128)(2,1)}), bf16[32,64,256]{2,0,1:T(8,128)(2,1)S(1)}, u32[]{:S(2)}, u32[]{:S(2)}) %all-to-all-start) | async-done | bytes 1048608 | tf_op jit(solution)/shard_map/all_to_all | solution.py:49
  52.2 0.4 fusion.8
  52.6 0.4 fusion
  53.0 1.1 divide_convert_fusion.1
  54.1 43.6 %all_to_all.29 = bf16[64,32,256]{2,1,0:T(8,128)(2,1)S(1)} all-to-all(bf16[64,32,256]{2,1,0:T(8,128)(2,1)S(1)} %bitcast.61), channel_id=1, replica_groups=mesh['lon_0'=4,'lon_1'=2,'lon_2'=8,'lat_0'=4,'lat_1'=2] {'lon_0','lon_1'..., dimensions={0} | all-to-all | bytes 2097152 | tf_op jit(solution)/shard_map/all_to_all | solution.py:65
  97.8 1.6 copy.31
  99.3 6.6 %collective-permute-start.2 = (bf16[32,64,256]{2,1,0:T(8,128)(2,1)}, bf16[32,64,256]{2,1,0:T(8,128)(2,1)}, u32[]{:S(2)}, u32[]{:S(2)}) collective-permute-start(bf16[32,64,256]{2,1,0:T(8,128)(2,1)} %bitcast.53), channel_id=1, source_target_pairs={{0,2},{1,3},{2,4},{3,5},{4,6},{5,7},{8,10},{9,11},{10,12},{11,13},... | collective-permute-start | bytes 3145736 | tf_op jit(solution)/shard_map/ppermute | solution.py:16
  106.0 3.3 %collective-permute-start.1 = (bf16[32,64,256]{2,1,0:T(8,128)(2,1)}, bf16[32,64,256]{2,1,0:T(8,128)(2,1)S(1)}, u32[]{:S(2)}, u32[]{:S(2)}) collective-permute-start(bf16[32,64,256]{2,1,0:T(8,128)(2,1)} %bitcast.53), channel_id=1, source_target_pairs={{1,0},{2,1},{3,2},{4,3},{5,4},{6,5},{7,6},{9,8},{10,9},{11,10},{12... | collective-permute-start | bytes 3145736 | tf_op jit(solution)/shard_map/ppermute | solution.py:16
  109.3 2.2 %collective-permute-start = (bf16[32,64,256]{2,1,0:T(8,128)(2,1)}, bf16[32,64,256]{2,1,0:T(8,128)(2,1)S(1)}, u32[]{:S(2)}, u32[]{:S(2)}) collective-permute-start(bf16[32,64,256]{2,1,0:T(8,128)(2,1)} %bitcast.53), channel_id=1, source_target_pairs={{0,1},{1,2},{2,3},{3,4},{4,5},{5,6},{6,7},{8,9},{9,10},{10,11},{11... | collective-permute-start | bytes 3145736 | tf_op jit(solution)/shard_map/ppermute | solution.py:16
  111.7 1.3 collective-permute-start.3
  113.0 0.9 fusion.20
  113.9 12.7 %collective-permute-done.2 = bf16[32,64,256]{2,1,0:T(8,128)(2,1)} collective-permute-done((bf16[32,64,256]{2,1,0:T(8,128)(2,1)}, bf16[32,64,256]{2,1,0:T(8,128)(2,1)}, u32[]{:S(2)}, u32[]{:S(2)}) %collective-permute-start.2) | collective-permute-done | bytes 1048608 | tf_op jit(solution)/shard_map/ppermute | solution.py:16
  126.6 1.6 fusion.14
  128.3 0.4 fusion.16
  128.8 10.7 %collective-permute-done = bf16[32,64,256]{2,1,0:T(8,128)(2,1)S(1)} collective-permute-done((bf16[32,64,256]{2,1,0:T(8,128)(2,1)}, bf16[32,64,256]{2,1,0:T(8,128)(2,1)S(1)}, u32[]{:S(2)}, u32[]{:S(2)}) %collective-permute-start) | collective-permute-done | bytes 1048608 | tf_op jit(solution)/shard_map/ppermute | solution.py:16
  139.5 0.4 fusion.18
  139.9 0.7 fusion.7
  140.6 0.9 reshape.78
  141.5 0.7 fusion.70
  142.2 9.1 %all-gather = f32[256,64]{1,0:T(8,128)S(1)} all-gather(f32[64,64]{1,0:T(8,128)S(1)} %fusion.70), channel_id=2, replica_groups=mesh['lon_0'=4,'lon_1'=2,'lon_2'=8,'lat_0'=4,'lat_1'=2] {'lon_0'}, dimensions={0}, use_global_device_ids=true | all-gather | bytes 81920 | tf_op jit(solution)/shard_map/all_gather | solution.py:21
  151.3 7.3 %all-gather.1 = f32[128,64]{1,0:T(8,128)S(1)} all-gather(f32[64,64]{1,0:T(8,128)S(1)} %reduce_sum.65), channel_id=3, replica_groups=mesh['lon_0'=4,'lon_1'=2,'lon_2'=8,'lat_0'=4,'lat_1'=2] {'lon_1'}, dimensions={0}, use_global_device_ids=true | all-gather | bytes 49152 | tf_op jit(solution)/shard_map/all_gather | solution.py:21
  158.7 18.7 %all-gather.2 = f32[512,64]{1,0:T(8,128)S(1)} all-gather(f32[64,64]{1,0:T(8,128)S(1)} %reduce_sum.66), channel_id=4, replica_groups=mesh['lon_0'=4,'lon_1'=2,'lon_2'=8,'lat_0'=4,'lat_1'=2] {'lon_2'}, dimensions={0}, use_global_device_ids=true | all-gather | bytes 147456 | tf_op jit(solution)/shard_map/all_gather | solution.py:21
  177.4 10.5 %all-gather.3 = f32[256,64]{1,0:T(8,128)S(1)} all-gather(f32[64,64]{1,0:T(8,128)S(1)} %reduce_sum.67), channel_id=5, replica_groups=mesh['lon_0'=4,'lon_1'=2,'lon_2'=8,'lat_0'=4,'lat_1'=2] {'lat_0'}, dimensions={0}, use_global_device_ids=true | all-gather | bytes 81920 | tf_op jit(solution)/shard_map/all_gather | solution.py:21
  187.9 20.1 %all-gather.4 = f32[128,64]{1,0:T(8,128)S(1)} all-gather(f32[64,64]{1,0:T(8,128)S(1)} %reduce_sum.68), channel_id=6, replica_groups=mesh['lon_0'=4,'lon_1'=2,'lon_2'=8,'lat_0'=4,'lat_1'=2] {'lat_1'}, dimensions={0}, use_global_device_ids=true | all-gather | bytes 49152 | tf_op jit(solution)/shard_map/all_gather | solution.py:21
  208.1 0.6 broadcast_multiply_fusion
  (16 shorter events, 1.2 us)
Async XLA Ops:
  2.4 1.2 copy-start
  6.2 45.7 %all-to-all-start = ((bf16[32,64,256]{2,0,1:T(8,128)(2,1)}), bf16[32,64,256]{2,0,1:T(8,128)(2,1)S(1)}, u32[]{:S(2)}, u32[]{:S(2)}) async-start(bf16[32,64,256]{2,0,1:T(8,128)(2,1)} %multiply_convert_fusion), calls=%async_computation | async-start | bytes 2097152 | tf_op jit(solution)/shard_map/all_to_all | solution.py:49
  99.3 27.3 %collective-permute-start.2 = (bf16[32,64,256]{2,1,0:T(8,128)(2,1)}, bf16[32,64,256]{2,1,0:T(8,128)(2,1)}, u32[]{:S(2)}, u32[]{:S(2)}) collective-permute-start(bf16[32,64,256]{2,1,0:T(8,128)(2,1)} %bitcast.53), channel_id=1, source_target_pairs={{0,2},{1,3},{2,4},{3,5},{4,6},{5,7},{8,10},{9,11},{10,12},{11,13},... | collective-permute-start | bytes 3145736 | tf_op jit(solution)/shard_map/ppermute | solution.py:16
  106.0 22.4 %collective-permute-start.1 = (bf16[32,64,256]{2,1,0:T(8,128)(2,1)}, bf16[32,64,256]{2,1,0:T(8,128)(2,1)S(1)}, u32[]{:S(2)}, u32[]{:S(2)}) collective-permute-start(bf16[32,64,256]{2,1,0:T(8,128)(2,1)} %bitcast.53), channel_id=1, source_target_pairs={{1,0},{2,1},{3,2},{4,3},{5,4},{6,5},{7,6},{9,8},{10,9},{11,10},{12... | collective-permute-start | bytes 3145736 | tf_op jit(solution)/shard_map/ppermute | solution.py:16
  109.3 30.2 %collective-permute-start = (bf16[32,64,256]{2,1,0:T(8,128)(2,1)}, bf16[32,64,256]{2,1,0:T(8,128)(2,1)S(1)}, u32[]{:S(2)}, u32[]{:S(2)}) collective-permute-start(bf16[32,64,256]{2,1,0:T(8,128)(2,1)} %bitcast.53), channel_id=1, source_target_pairs={{0,1},{1,2},{2,3},{3,4},{4,5},{5,6},{6,7},{8,9},{9,10},{10,11},{11... | collective-permute-start | bytes 3145736 | tf_op jit(solution)/shard_map/ppermute | solution.py:16
  111.7 28.2 %collective-permute-start.3 = (bf16[32,64,256]{2,1,0:T(8,128)(2,1)}, bf16[32,64,256]{2,1,0:T(8,128)(2,1)S(1)}, u32[]{:S(2)}, u32[]{:S(2)}) collective-permute-start(bf16[32,64,256]{2,1,0:T(8,128)(2,1)} %bitcast.53), channel_id=1, source_target_pairs={{2,0},{3,1},{4,2},{5,3},{6,4},{7,5},{10,8},{11,9},{12,10},{13,11},... | collective-permute-start | bytes 3145736 | tf_op jit(solution)/shard_map/ppermute | solution.py:16
  140.6 1.6 copy-start.1
